TPU v7x, 256 devices: a whole 4x4x8 slice. The times are simulated.
256 devices in a mesh: obs: 32 (over z, x_hi, core), ind: 8 (over y, x_lo).
Axes of the slice: x: 4 (x_hi: 2, x_lo: 2; x = x_hi * 2 + x_lo), y: 4, z: 8, core: 2. Of those that a mesh axis runs over, the one named last changes fastest.
Arguments:
- obs_coords: float32 [2, 131072], P(None, 'obs'), may hold values from 0 to 1
- obs_codes: int32 [131072], P('obs'), may hold values from 0 to 47
- route_plan: int32 [32, 32], replicated, may hold values from 0 to 1, as said below
- inducing_coords: float32 [2, 8192], P(None, 'ind'), may hold values from 0 to 1
- inducing_bands: int32 [8192], P('ind'), may hold values from 0 to 5
- band_mix: float32 [6, 6], replicated, may hold values from -2.4 to 2.4
- lengthscales: float32 [2], replicated, may hold values from 0.04 to 0.1
- class_scales: float32 [8], replicated, may hold values from 0.5 to 2
- prior_factor: bfloat16 [8192, 1024], P(('ind', 'obs')), may hold values from -0.046875 to 0.046875
- variational_chol: bfloat16 [8192, 1024], P(('ind', 'obs')), may hold values from -1 to 1, as said below
- variational_mean: bfloat16 [8, 8192], P(None, 'ind'), may hold values from -6 to 6
Outputs:
- class_probs: float32 [8, 65536], P(None, 'obs')
- grad_chol: float32 [8192, 1024], P(('ind', 'obs'))
- grad_mean: float32 [8, 8192], P(None, 'ind')
Inputs may be any that keep to these rules, and one draw needn't show every extreme that they name: `route_plan`: entry [s, d] is the number of 128-row blocks that reader s hands to device d; every column sums to 16; a reader's blocks go out in order of destination from the front of its buffer. `variational_chol`: each block's rows are lower triangular within the block, with diagonal entries of 0.3 to 1.
All inputs are finite; a program needn't handle non-finite values.
Results may differ from a plain program's by a relative error of at most 0.014.
Values may be sent and summed in bfloat16 or wider, within the bound.
A program may use at most 64 MiB of HBM per device.

v0:
```python
import jax
import jax.numpy as jnp
from jax import lax
from jax.sharding import PartitionSpec as P

C = 8
NB = 6
ROWS_DEV = 2048
precise = lax.Precision.HIGHEST


def cross_cov(coords, band_ids, centers, center_bands, lengthscales, coupling):
    delta_t = (coords[0][:, None] - centers[0][None, :]) / lengthscales[0]
    delta_w = (coords[1][:, None] - centers[1][None, :]) / lengthscales[1]
    kinds = jnp.arange(NB, dtype=jnp.int32)
    row_hot = (band_ids[:, None] == kinds[None, :]).astype(jnp.float32)
    col_hot = (center_bands[:, None] == kinds[None, :]).astype(jnp.float32)
    mixing = jnp.dot(jnp.dot(row_hot, coupling, precision=precise), col_hot.T, precision=precise)
    return (jnp.exp(-0.5 * (delta_t * delta_t + delta_w * delta_w)) * mixing).astype(jnp.bfloat16)


def likelihood(mean_sum, variance, class_scales):
    logits = mean_sum + 0.5 * class_scales[:, None] * variance[None, :]
    weights = jnp.exp(logits)
    chances = weights / jnp.sum(weights, axis=0, keepdims=True)
    var_slope = -0.5 * jnp.sum(chances * class_scales[:, None], axis=0)
    return (chances, var_slope)


def body(
    obs_coords,
    obs_codes,
    route_plan,
    inducing_coords,
    inducing_bands,
    band_mix,
    lengthscales,
    class_scales,
    prior_factor,
    variational_chol,
    variational_mean,
):
    devices = lax.axis_size("obs")
    my_index = lax.axis_index("obs")
    slot_rows = 128
    blocks = route_plan * slot_rows
    send_start = jnp.cumsum(blocks, axis=1) - blocks
    recv_start = jnp.cumsum(blocks, axis=0) - blocks
    my_sends = lax.dynamic_index_in_dim(send_start, my_index, 0, keepdims=False)
    my_recvs = lax.dynamic_index_in_dim(recv_start, my_index, 1, keepdims=False)
    stacked = jnp.concatenate([obs_coords, obs_codes.astype(jnp.float32)[None, :]], axis=0)
    padded = jnp.concatenate([stacked, jnp.zeros((3, slot_rows), jnp.float32)], axis=1)
    outgoing = jax.vmap(lambda offset: lax.dynamic_slice_in_dim(padded, offset, slot_rows, 1))(
        my_sends
    )
    incoming = lax.all_to_all(outgoing, "obs", split_axis=0, concat_axis=0, tiled=True)
    position = jnp.arange(ROWS_DEV, dtype=jnp.int32)
    sources = jnp.arange(devices, dtype=jnp.int32)
    source = jnp.sum((my_recvs[None, :] <= position[:, None]).astype(jnp.int32), axis=1) - 1
    pick = (source[:, None] == sources[None, :]).astype(jnp.int32)
    begin_row = jnp.sum(pick * my_recvs[None, :], axis=1)
    arrived = incoming[source, :, position - begin_row].T
    coords = arrived[0:2]
    code_ids = arrived[2].astype(jnp.int32)
    band_ids = code_ids % NB
    labels = code_ids // NB
    coupling = jnp.eye(NB, dtype=jnp.float32) + jnp.dot(band_mix, band_mix.T, precision=precise)
    kinds = jnp.arange(NB, dtype=jnp.int32)
    row_hot = (band_ids[:, None] == kinds[None, :]).astype(jnp.float32)
    self_cov = jnp.sum(row_hot * jnp.dot(row_hot, coupling, precision=precise), axis=1)
    kernel_rows = cross_cov(
        coords, band_ids, inducing_coords, inducing_bands, lengthscales, coupling
    )
    prior_block, chol_block = (
        lax.all_gather(prior_factor, "obs", axis=0, tiled=True),
        lax.all_gather(variational_chol, "obs", axis=0, tiled=True),
    )
    whitened = jnp.dot(kernel_rows, prior_block, preferred_element_type=jnp.float32)
    whitened_bf = whitened.astype(jnp.bfloat16)
    covariant = jnp.dot(whitened_bf, chol_block, preferred_element_type=jnp.float32)
    mean_part = lax.dot_general(
        variational_mean, whitened_bf, (((1,), (1,)), ((), ())), preferred_element_type=jnp.float32
    )
    var_part = (jnp.sum(covariant * covariant, axis=1) - jnp.sum(whitened * whitened, axis=1))[
        None, :
    ]
    mean_sum, var_sum = lax.psum((mean_part, var_part), "ind")
    chances, var_slope = likelihood(mean_sum, self_cov + var_sum[0], class_scales)
    classes = jnp.arange(C, dtype=jnp.int32)
    mean_slope = ((labels[None, :] == classes[:, None]).astype(jnp.float32) - chances).astype(
        jnp.bfloat16
    )
    heavy = (2.0 * var_slope[:, None] * covariant).astype(jnp.bfloat16)
    piece_rows = variational_chol.shape[0]
    full_width = variational_chol.shape[1]
    column_ids = jnp.arange(full_width, dtype=jnp.int32)
    own_rows = my_index * piece_rows + jnp.arange(piece_rows, dtype=jnp.int32)[:, None]
    term = lax.dot_general(
        whitened_bf, heavy, (((0,), (0,)), ((), ())), preferred_element_type=jnp.float32
    )
    row_ids = jnp.arange(lax.axis_size("obs") * piece_rows, dtype=jnp.int32)[:, None]
    data_term = lax.psum_scatter(
        jnp.where(column_ids[None, :] <= row_ids, term, 0.0).astype(jnp.bfloat16),
        "obs",
        scatter_dimension=0,
        tiled=True,
    ).astype(jnp.float32)
    on_diag = column_ids[None, :] == own_rows
    own_chol = variational_chol.astype(jnp.float32)
    diagonal = jnp.sum(jnp.where(on_diag, own_chol, 0.0), axis=1, keepdims=True)
    grad_chol = data_term - own_chol + jnp.where(on_diag, 1.0 / diagonal, 0.0)
    mean_term = lax.dot_general(
        mean_slope, whitened_bf, (((1,), (0,)), ((), ())), preferred_element_type=jnp.float32
    )
    grad_mean = lax.psum(mean_term, "obs") - variational_mean.astype(jnp.float32)
    return (chances, grad_chol, grad_mean)


def solution(mesh):
    placed = (
        P(None, "obs"),
        P("obs"),
        P(),
        P(None, "ind"),
        P("ind"),
        P(),
        P(),
        P(),
        P(("ind", "obs"), None),
        P(("ind", "obs"), None),
        P(None, "ind"),
    )
    return jax.shard_map(
        body,
        mesh=mesh,
        in_specs=placed,
        out_specs=(P(None, "obs"), P(("ind", "obs"), None), P(None, "ind")),
        check_vma=False,
    )
```

profile of v0, /device:TPU:8, one launch (start us, length us, event | category | flops | bytes accessed | tf_op | source)
XLA Modules:
  0.0 403.3 jit_solution(5778186779938577042)
XLA Ops:
  10.4 60.4 %while.1 = (s32[]{:T(128)}, f32[3,4224]{1,0:T(4,128)S(1)}, s32[32,2]{0,1:T(2,128)S(1)}, f32[32,3,128]{2,1,0:T(4,128)}, s32[]{:T(128)}) while((s32[]{:T(128)}, f32[3,4224]{1,0:T(4,128)S(1)}, s32[32,2]{0,1:T(2,128)S(1)}, f32[32,3,128]{2,1,0:T(4,128)}, s32[]{:T(128)}) %tuple.31), condition=%wide.while_cond, body=%wide.while_body.sunk | while | flops 2 | bytes 4197 | solution.py:53
  11.0 1.3 bitcast_dynamic-update-slice_fusion.2
  12.9 1.3 bitcast_dynamic-update-slice_fusion.2
  14.8 1.3 bitcast_dynamic-update-slice_fusion.2
  16.6 1.3 bitcast_dynamic-update-slice_fusion.2
  18.5 1.3 bitcast_dynamic-update-slice_fusion.2
  20.4 1.3 bitcast_dynamic-update-slice_fusion.2
  22.3 1.3 bitcast_dynamic-update-slice_fusion.2
  24.2 1.3 bitcast_dynamic-update-slice_fusion.2
  26.1 1.3 bitcast_dynamic-update-slice_fusion.2
  28.0 1.3 bitcast_dynamic-update-slice_fusion.2
  29.9 1.3 bitcast_dynamic-update-slice_fusion.2
  31.7 1.3 bitcast_dynamic-update-slice_fusion.2
  33.6 1.3 bitcast_dynamic-update-slice_fusion.2
  43.1 1.3 bitcast_dynamic-update-slice_fusion.2
  46.8 1.3 bitcast_dynamic-update-slice_fusion.2
  50.6 1.3 bitcast_dynamic-update-slice_fusion.2
  70.8 11.3 %all-to-all-start = ((f32[32,3,128]{2,1,0:T(4,128)}), f32[32,3,128]{2,1,0:T(4,128)S(1)}, u32[]{:S(2)}, u32[]{:S(2)}) async-start(f32[32,3,128]{2,1,0:T(4,128)} %get-tuple-element.10), calls=%async_computation | async-start | bytes 131072 | tf_op jit(solution)/shard_map/all_to_all | solution.py:56
  85.0 1.3 fusion.24
  86.4 5.7 %all-to-all-done = f32[32,3,128]{2,1,0:T(4,128)S(1)} async-done(((f32[32,3,128]{2,1,0:T(4,128)}), f32[32,3,128]{2,1,0:T(4,128)S(1)}, u32[]{:S(2)}, u32[]{:S(2)}) %all-to-all-start) | async-done | bytes 49184 | tf_op jit(solution)/shard_map/all_to_all | solution.py:56
  92.7 13.0 %gather_fusion = f32[2048,3]{1,0:T(8,128)S(1)} fusion(f32[32,3,128]{1,2,0:T(8,128)S(1)} %copy.17, s32[2048]{0:T(1024)S(1)} %bitcast.38), kind=kCustom, calls=%fused_computation | custom fusion | bytes 65536 | tf_op jit(solution)/shard_map/gather | solution.py:62
  108.2 10.1 %multiply_convert_fusion.1 = bf16[2048,1024]{1,0:T(8,128)(2,1)} fusion(f32[2048,6]{0,1:T(8,128)S(1)} %get-tuple-element.35, f32[]{:T(128)} %bitcast.10, f32[1024]{0:T(1024)S(1)} %bitcast.50, f32[2048]{0:T(1024)S(1)} %get-tuple-element.14, f32[]{:T(128)} %bitcast.8, f32[1024]{0:T(1024)S(1)} %bitcast.49, f32[2048]{0:T(1024)S(1)} %get-tuple-element.13, ...), kind=kOutput, calls=%fused_computation.6 | convolution fusion | flops 171972608 | bytes 4272136 | tf_op jit(solution)/shard_map/dot_general | solution.py:18
  118.3 7.5 %multiply_reduce_fusion = (f32[2048]{0:T(1024)S(1)}, bf16[2048,1024]{0,1:T(8,128)(2,1)S(1)}) fusion(bf16[2048,1024]{1,0:T(8,128)(2,1)} %multiply_convert_fusion.1, bf16[1024,1024]{1,0:T(8,128)(2,1)} %all-gather.3.cloned.1.call-done), kind=kOutput, calls=%fused_computation.4 | convolution fusion | flops 4301256704 | bytes 10493952 | tf_op jit(solution)/shard_map/dot_general | solution.py:78
  125.8 2.0 copy-done.1
  129.3 44.1 %all-gather.5.cloned.1.call-done = bf16[1024,1024]{1,0:T(8,128)(2,1)} async-done(((bf16[32,1024]{1,0:T(8,128)(2,1)}), bf16[1024,1024]{1,0:T(8,128)(2,1)}) %all-gather.5.cloned.1.call-update) | async-done | bytes 2097168 | tf_op jit(solution)/shard_map/all_gather | solution.py:76
  173.4 10.7 %multiply_reduce_fusion.1 = (f32[2048]{0:T(1024)S(1)}, f32[2048,1024]{0,1:T(8,128)}) fusion(bf16[2048,1024]{0,1:T(8,128)(2,1)} %copy-done.1, bf16[1024,1024]{1,0:T(8,128)(2,1)} %all-gather.5.cloned.1.call-done), kind=kOutput, calls=%fused_computation.5 | convolution fusion | flops 4299159552 | bytes 14688256 | tf_op jit(solution)/shard_map/dot_general | solution.py:80
  184.0 16.9 %psum.22 = f32[1,2048]{1,0:T(1,128)S(1)} all-reduce(f32[1,2048]{1,0:T(1,128)S(1)} %bitcast.45), channel_id=1, replica_groups=mesh['obs'=32,'ind'=8] {'ind'}, use_global_device_ids=true, to_apply=%region_8.9 | all-reduce | flops 2048 | bytes 16384 | tf_op jit(solution)/shard_map/psum | solution.py:87
  201.0 48.5 %all-reduce.4.cloned.1.call-done = f32[8,2048]{1,0:T(8,128)} async-done(((f32[8,2048]{1,0:T(8,128)}), f32[8,2048]{1,0:T(8,128)}) %all-reduce.4.cloned.1.call-update) | async-done | bytes 65552 | tf_op jit(solution)/shard_map/psum | solution.py:87
  251.4 10.7 %select_convert_fusion = bf16[1024,1024]{1,0:T(8,128)(2,1)} fusion(bf16[2048,1024]{0,1:T(8,128)(2,1)} %copy-done.1, f32[2048,1024]{0,1:T(8,128)} %get-tuple-element.37, f32[2048]{0:T(1024)S(1)} %broadcast_multiply_fusion.1), kind=kOutput, calls=%fused_computation.8 | convolution fusion | flops 4302307328 | bytes 14688256 | tf_op jit(solution)/shard_map/dot_general | solution.py:98
  262.3 3.4 fusion.12
  265.7 128.9 %psum.23 = f32[8,1024]{1,0:T(8,128)S(1)} all-reduce(f32[8,1024]{1,0:T(8,128)S(1)} %fusion.12), channel_id=1, replica_groups=mesh['obs'=32,'ind'=8] {'obs'}, use_global_device_ids=true, to_apply=%region_13.14 | all-reduce | flops 8192 | bytes 65536 | tf_op jit(solution)/shard_map/psum | solution.py:115
  395.2 1.6 fusion.7
  (134 shorter events, 52.9 us)
Async XLA Ops:
  7.2 76.2 %copy-start = (f32[6,6]{1,0:T(8,128)S(1)}, f32[6,6]{1,0:T(8,128)}, u32[]{:S(2)}) copy-start(f32[6,6]{1,0:T(8,128)} %param.16) | copy-start | bytes 436
  7.2 111.1 %all-gather.3.cloned.1.call-start = ((), (), s32[]{:S(2)}) async-start(), calls=%async_computation.2 | async-start | bytes 2162688 | tf_op jit(solution)/shard_map/all_gather | solution.py:75
  70.8 21.3 %all-to-all-start = ((f32[32,3,128]{2,1,0:T(4,128)}), f32[32,3,128]{2,1,0:T(4,128)S(1)}, u32[]{:S(2)}, u32[]{:S(2)}) async-start(f32[32,3,128]{2,1,0:T(4,128)} %get-tuple-element.10), calls=%async_computation | async-start | bytes 131072 | tf_op jit(solution)/shard_map/all_to_all | solution.py:56
  82.1 91.3 %all-gather.5.cloned.1.call-start = ((), (), s32[]{:S(2)}) async-start(), calls=%async_computation.4 | async-start | bytes 2162688 | tf_op jit(solution)/shard_map/all_gather | solution.py:76
  82.9 166.6 %all-reduce.4.cloned.1.call-start = ((), (), s32[]{:S(2)}) async-start(), calls=%async_computation.3 | async-start | bytes 131072 | tf_op jit(solution)/shard_map/psum | solution.py:87
  92.7 15.5 %copy-start.6 = (s32[1024]{0:T(1024)S(1)}, s32[1024]{0:T(1024)}, u32[]{:S(2)}) copy-start(s32[1024]{0:T(1024)} %param.15) | copy-start | bytes 12292
  118.3 9.5 %copy-start.4 = (bf16[8,1024]{1,0:T(8,128)(2,1)S(1)}, bf16[8,1024]{1,0:T(8,128)(2,1)}, u32[]{:S(2)}) copy-start(bf16[8,1024]{1,0:T(8,128)(2,1)} %param.21) | copy-start | bytes 49156
  125.8 2.0 copy-start.1
  129.1 121.3 %copy-start.5 = (f32[8]{0:T(128)S(1)}, f32[8]{0:T(128)}, u32[]{:S(2)}) copy-start(f32[8]{0:T(128)} %param.18) | copy-start | bytes 100
  129.1 266.1 %reduce-scatter.2.cloned.1.call-start = ((), (), s32[]{:S(2)}) async-start(), calls=%async_computation.5 | async-start | bytes 2162688 | tf_op jit(solution)/shard_map/reduce_scatter | solution.py:102
  251.4 10.9 %copy-start.3 = (f32[8,2048]{1,0:T(8,128)}, f32[8,2048]{1,0:T(8,128)S(1)}, u32[]{:S(2)}) copy-start(f32[8,2048]{1,0:T(8,128)S(1)} %get-tuple-element.24) | copy-start | bytes 196612
  251.4 10.7 %copy-start.2 = (bf16[32,1024]{1,0:T(8,128)(2,1)S(1)}, bf16[32,1024]{1,0:T(8,128)(2,1)}, u32[]{:S(2)}) copy-start(bf16[32,1024]{1,0:T(8,128)(2,1)} %param.20) | copy-start | bytes 196612
Sparse Core Ops, SparseCore 0:
  10.8 82.8 all-gather.2
  96.5 76.8 all-gather.4
  176.6 72.8 all-reduce.3
  262.2 120.2 reduce-scatter.1
where the time goes:
time: 405 us; the launch traced here: 403 us
  blocking collectives  146 us (36%)
  waiting for transfers between devices  99.7 us (25%)
  local copies, waits for them, and re-layouts  79.1 us (20%)
  matrix products  43.9 us (11%)
  between operations  14 us (3%)
  starting transfers between devices  11.7 us (3%)
  other arithmetic  9.17 us (2%)
    psum x1, blocking collectives, body(): lax.psum(mean_term, 'obs') - variational_mean.astype(jnp.float32)  129 us
    gather x96, local copies, waits for them, and re-layouts  60.4 us
    psum x1, waiting for transfers between devices, body(): mean_sum, var_sum = lax.psum((mean_part, var_part), 'ind')  48.5 us
    all_gather x1, waiting for transfers between devices, body(): lax.all_gather(variational_chol, 'obs', axis=0, tiled=True)  44.1 us
    psum x1, blocking collectives, body(): mean_sum, var_sum = lax.psum((mean_part, var_part), 'ind')  16.9 us
    gather x1, local copies, waits for them, and re-layouts, body(): arrived = incoming[source, :, position - begin_row].T  13 us
    all_to_all x1, starting transfers between devices, body(): lax.all_to_all(outgoing, 'obs', split_axis=0, concat_axis=0, tiled=True)  11.3 us
    dot_general x1, matrix products, body(): lax.dot_general(whitened_bf, heavy, (((0,), (0,)), ((), ())), preferred_e...  10.7 us
  transfers between devices with their start and end apart: 5, of which 3 were waited for; matrix products, arithmetic and copies ran while one was open for 29% of the time, Pallas kernels for 0%

commit v1 on v0

--- a/solution.py
+++ b/solution.py
@@ -112,7 +112,9 @@
     mean_term = lax.dot_general(
         mean_slope, whitened_bf, (((1,), (0,)), ((), ())), preferred_element_type=jnp.float32
     )
-    grad_mean = lax.psum(mean_term, "obs") - variational_mean.astype(jnp.float32)
+    grad_mean = jnp.sum(lax.all_gather(mean_term, "obs"), axis=0) - variational_mean.astype(
+        jnp.float32
+    )
     return (chances, grad_chol, grad_mean)
 
 

time: 405 us -> 464 us (1.15)
  waiting for transfers between devices: 99.7 us -> 286 us
  blocking collectives: 146 us -> 16.9 us
    psum x1 -> x0, blocking collectives: 129 us -> none  [body(): lax.psum(mean_term, 'obs') - variational_mean.astype(jnp.float32)]
    reduce_scatter x1, waiting for transfers between devices: 0.01 us -> 119 us  [body(): lax.psum_scatter(jnp.where(column_ids[None, :] <= row_ids, term, 0.0).ast...]
    all_gather x0 -> x1, waiting for transfers between devices: none -> 67.4 us  [body(): lax.all_gather(mean_term, 'obs')]
  transfers between devices with their start and end apart: 5 -> 6, of which waited for: 3 -> 5; matrix products, arithmetic and copies ran while one was open for 29% -> 27% of each run, Pallas kernels for 0% -> 0%
where the time goes in v1:
time: 464 us; the launch traced here: 463 us
  waiting for transfers between devices  286 us (62%)
  local copies, waits for them, and re-layouts  79.1 us (17%)
  matrix products  44.6 us (10%)
  blocking collectives  16.9 us (4%)
  between operations  14 us (3%)
  starting transfers between devices  11.7 us (3%)
  other arithmetic  10.5 us (2%)
    reduce_scatter x1, waiting for transfers between devices, body(): lax.psum_scatter(jnp.where(column_ids[None, :] <= row_ids, term, 0.0).ast...  119 us
    all_gather x1, waiting for transfers between devices, body(): lax.all_gather(mean_term, 'obs')  67.4 us
    gather x96, local copies, waits for them, and re-layouts  60.4 us
    psum x1, waiting for transfers between devices, body(): mean_sum, var_sum = lax.psum((mean_part, var_part), 'ind')  48.5 us
    all_gather x1, waiting for transfers between devices, body(): lax.all_gather(variational_chol, 'obs', axis=0, tiled=True)  44 us
    psum x1, blocking collectives, body(): mean_sum, var_sum = lax.psum((mean_part, var_part), 'ind')  16.9 us
    gather x1, local copies, waits for them, and re-layouts, body(): arrived = incoming[source, :, position - begin_row].T  13 us
    all_to_all x1, starting transfers between devices, body(): lax.all_to_all(outgoing, 'obs', split_axis=0, concat_axis=0, tiled=True)  11.3 us
  transfers between devices with their start and end apart: 6, of which 5 were waited for; matrix products, arithmetic and copies ran while one was open for 27% of the time, Pallas kernels for 0%

profile of v1, /device:TPU:8, one launch (start us, length us, event | category | flops | bytes accessed | tf_op | source)
XLA Modules:
  0.0 462.6 jit_solution(15563889690973314078)
XLA Ops:
  10.4 60.4 %while.1 = (s32[]{:T(128)}, f32[3,4224]{1,0:T(4,128)S(1)}, s32[32,2]{0,1:T(2,128)S(1)}, f32[32,3,128]{2,1,0:T(4,128)}, s32[]{:T(128)}) while((s32[]{:T(128)}, f32[3,4224]{1,0:T(4,128)S(1)}, s32[32,2]{0,1:T(2,128)S(1)}, f32[32,3,128]{2,1,0:T(4,128)}, s32[]{:T(128)}) %tuple.31), condition=%wide.while_cond, body=%wide.while_body.sunk | while | flops 2 | bytes 4197 | solution.py:53
  11.0 1.3 bitcast_dynamic-update-slice_fusion.2
  12.9 1.3 bitcast_dynamic-update-slice_fusion.2
  14.8 1.3 bitcast_dynamic-update-slice_fusion.2
  16.6 1.3 bitcast_dynamic-update-slice_fusion.2
  18.5 1.3 bitcast_dynamic-update-slice_fusion.2
  20.4 1.3 bitcast_dynamic-update-slice_fusion.2
  22.3 1.3 bitcast_dynamic-update-slice_fusion.2
  24.2 1.3 bitcast_dynamic-update-slice_fusion.2
  26.1 1.3 bitcast_dynamic-update-slice_fusion.2
  28.0 1.3 bitcast_dynamic-update-slice_fusion.2
  29.9 1.3 bitcast_dynamic-update-slice_fusion.2
  31.7 1.3 bitcast_dynamic-update-slice_fusion.2
  43.1 1.3 bitcast_dynamic-update-slice_fusion.2
  46.8 1.3 bitcast_dynamic-update-slice_fusion.2
  50.6 1.3 bitcast_dynamic-update-slice_fusion.2
  70.8 11.3 %all-to-all-start = ((f32[32,3,128]{2,1,0:T(4,128)}), f32[32,3,128]{2,1,0:T(4,128)S(1)}, u32[]{:S(2)}, u32[]{:S(2)}) async-start(f32[32,3,128]{2,1,0:T(4,128)} %get-tuple-element.10), calls=%async_computation | async-start | bytes 131072 | tf_op jit(solution)/shard_map/all_to_all | solution.py:56
  85.0 1.3 fusion.24
  86.4 5.7 %all-to-all-done = f32[32,3,128]{2,1,0:T(4,128)S(1)} async-done(((f32[32,3,128]{2,1,0:T(4,128)}), f32[32,3,128]{2,1,0:T(4,128)S(1)}, u32[]{:S(2)}, u32[]{:S(2)}) %all-to-all-start) | async-done | bytes 49184 | tf_op jit(solution)/shard_map/all_to_all | solution.py:56
  92.7 13.0 %gather_fusion = f32[2048,3]{1,0:T(8,128)S(1)} fusion(f32[32,3,128]{1,2,0:T(8,128)S(1)} %copy.17, s32[2048]{0:T(1024)S(1)} %bitcast.40), kind=kCustom, calls=%fused_computation | custom fusion | bytes 65536 | tf_op jit(solution)/shard_map/gather | solution.py:62
  108.2 10.1 %multiply_convert_fusion.1 = bf16[2048,1024]{1,0:T(8,128)(2,1)} fusion(f32[2048,6]{0,1:T(8,128)S(1)} %get-tuple-element.35, f32[]{:T(128)} %bitcast.10, f32[1024]{0:T(1024)S(1)} %bitcast.52, f32[2048]{0:T(1024)S(1)} %get-tuple-element.14, f32[]{:T(128)} %bitcast.8, f32[1024]{0:T(1024)S(1)} %bitcast.51, f32[2048]{0:T(1024)S(1)} %get-tuple-element.13, ...), kind=kOutput, calls=%fused_computation.6 | convolution fusion | flops 171972608 | bytes 4272136 | tf_op jit(solution)/shard_map/dot_general | solution.py:18
  118.3 7.5 %multiply_reduce_fusion = (f32[2048]{0:T(1024)S(1)}, bf16[2048,1024]{0,1:T(8,128)(2,1)S(1)}) fusion(bf16[2048,1024]{1,0:T(8,128)(2,1)} %multiply_convert_fusion.1, bf16[1024,1024]{1,0:T(8,128)(2,1)} %all-gather.5.cloned.1.call-done), kind=kOutput, calls=%fused_computation.4 | convolution fusion | flops 4301256704 | bytes 10493952 | tf_op jit(solution)/shard_map/dot_general | solution.py:78
  125.8 2.0 copy-done.1
  129.3 44.0 %all-gather.7.cloned.1.call-done = bf16[1024,1024]{1,0:T(8,128)(2,1)} async-done(((bf16[32,1024]{1,0:T(8,128)(2,1)}), bf16[1024,1024]{1,0:T(8,128)(2,1)}) %all-gather.7.cloned.1.call-update) | async-done | bytes 2097168 | tf_op jit(solution)/shard_map/all_gather | solution.py:76
  173.4 10.7 %multiply_reduce_fusion.1 = (f32[2048]{0:T(1024)S(1)}, f32[2048,1024]{0,1:T(8,128)}) fusion(bf16[2048,1024]{0,1:T(8,128)(2,1)} %copy-done.1, bf16[1024,1024]{1,0:T(8,128)(2,1)} %all-gather.7.cloned.1.call-done), kind=kOutput, calls=%fused_computation.5 | convolution fusion | flops 4299159552 | bytes 14688256 | tf_op jit(solution)/shard_map/dot_general | solution.py:80
  184.0 16.9 %psum.15 = f32[1,2048]{1,0:T(1,128)S(1)} all-reduce(f32[1,2048]{1,0:T(1,128)S(1)} %bitcast.47), channel_id=1, replica_groups=mesh['obs'=32,'ind'=8] {'ind'}, use_global_device_ids=true, to_apply=%region_8.9 | all-reduce | flops 2048 | bytes 16384 | tf_op jit(solution)/shard_map/psum | solution.py:87
  201.0 48.5 %all-reduce.4.cloned.1.call-done = f32[8,2048]{1,0:T(8,128)} async-done(((f32[8,2048]{1,0:T(8,128)}), f32[8,2048]{1,0:T(8,128)}) %all-reduce.4.cloned.1.call-update) | async-done | bytes 65552 | tf_op jit(solution)/shard_map/psum | solution.py:87
  251.4 4.0 fusion.12
  255.5 10.7 %select_convert_fusion = bf16[1024,1024]{1,0:T(8,128)(2,1)} fusion(bf16[2048,1024]{0,1:T(8,128)(2,1)} %copy-done.1, f32[2048,1024]{0,1:T(8,128)} %get-tuple-element.37, f32[2048]{0:T(1024)S(1)} %broadcast_multiply_fusion.1), kind=kOutput, calls=%fused_computation.8 | convolution fusion | flops 4302307328 | bytes 14688256 | tf_op jit(solution)/shard_map/dot_general | solution.py:98
  266.4 67.4 %all-gather.9.cloned.1.call-done = f32[256,1024]{1,0:T(8,128)} async-done(((f32[8,1024]{1,0:T(8,128)}), f32[256,1024]{1,0:T(8,128)}) %all-gather.9.cloned.1.call-update) | async-done | bytes 1048592 | tf_op jit(solution)/shard_map/all_gather | solution.py:115
  335.7 118.9 %reduce-scatter.2.cloned.1.call-done = bf16[32,1024]{1,0:T(8,128)(2,1)} async-done(((bf16[1024,1024]{1,0:T(8,128)(2,1)}), bf16[32,1024]{1,0:T(8,128)(2,1)}) %reduce-scatter.2.cloned.1.call-update) | async-done | bytes 65552 | tf_op jit(solution)/shard_map/reduce_scatter | solution.py:102
  454.5 1.6 fusion.7
  (137 shorter events, 55.6 us)
Async XLA Ops:
  7.2 76.2 %copy-start = (f32[6,6]{1,0:T(8,128)S(1)}, f32[6,6]{1,0:T(8,128)}, u32[]{:S(2)}) copy-start(f32[6,6]{1,0:T(8,128)} %param.16) | copy-start | bytes 436
  7.2 111.1 %all-gather.5.cloned.1.call-start = ((), (), s32[]{:S(2)}) async-start(), calls=%async_computation.2 | async-start | bytes 2162688 | tf_op jit(solution)/shard_map/all_gather | solution.py:75
  70.8 21.3 %all-to-all-start = ((f32[32,3,128]{2,1,0:T(4,128)}), f32[32,3,128]{2,1,0:T(4,128)S(1)}, u32[]{:S(2)}, u32[]{:S(2)}) async-start(f32[32,3,128]{2,1,0:T(4,128)} %get-tuple-element.10), calls=%async_computation | async-start | bytes 131072 | tf_op jit(solution)/shard_map/all_to_all | solution.py:56
  82.1 91.3 %all-gather.7.cloned.1.call-start = ((), (), s32[]{:S(2)}) async-start(), calls=%async_computation.4 | async-start | bytes 2162688 | tf_op jit(solution)/shard_map/all_gather | solution.py:76
  82.9 166.6 %all-reduce.4.cloned.1.call-start = ((), (), s32[]{:S(2)}) async-start(), calls=%async_computation.3 | async-start | bytes 131072 | tf_op jit(solution)/shard_map/psum | solution.py:87
  92.7 15.5 %copy-start.6 = (s32[1024]{0:T(1024)S(1)}, s32[1024]{0:T(1024)}, u32[]{:S(2)}) copy-start(s32[1024]{0:T(1024)} %param.15) | copy-start | bytes 12292
  118.3 9.5 %copy-start.4 = (bf16[8,1024]{1,0:T(8,128)(2,1)S(1)}, bf16[8,1024]{1,0:T(8,128)(2,1)}, u32[]{:S(2)}) copy-start(bf16[8,1024]{1,0:T(8,128)(2,1)} %param.21) | copy-start | bytes 49156
  125.8 2.0 copy-start.1
  129.1 121.3 %copy-start.5 = (f32[8]{0:T(128)S(1)}, f32[8]{0:T(128)}, u32[]{:S(2)}) copy-start(f32[8]{0:T(128)} %param.18) | copy-start | bytes 100
  129.1 204.7 %all-gather.9.cloned.1.call-start = ((), (), s32[]{:S(2)}) async-start(), calls=%async_computation.6 | async-start | bytes 1081344 | tf_op jit(solution)/shard_map/all_gather | solution.py:115
  251.4 14.8 %copy-start.3 = (f32[8,2048]{1,0:T(8,128)}, f32[8,2048]{1,0:T(8,128)S(1)}, u32[]{:S(2)}) copy-start(f32[8,2048]{1,0:T(8,128)S(1)} %get-tuple-element.24) | copy-start | bytes 196612
  255.4 199.1 %reduce-scatter.2.cloned.1.call-start = ((), (), s32[]{:S(2)}) async-start(), calls=%async_computation.5 | async-start | bytes 2162688 | tf_op jit(solution)/shard_map/reduce_scatter | solution.py:102
  255.5 10.7 %copy-start.2 = (bf16[32,1024]{1,0:T(8,128)(2,1)S(1)}, bf16[32,1024]{1,0:T(8,128)(2,1)}, u32[]{:S(2)}) copy-start(bf16[32,1024]{1,0:T(8,128)(2,1)} %param.20) | copy-start | bytes 196612
Sparse Core Ops, SparseCore 0:
  10.8 82.8 all-gather.4
  96.5 76.8 all-gather.6
  176.6 72.8 all-reduce.3
  255.5 78.1 all-gather.8
  338.3 116.1 reduce-scatter.1
